TPU v7x, 256 devices: a whole 4x4x8 slice. The times are simulated.
256 devices in a mesh: hid: 4 (over x_lo, core), tok: 64 (over x_hi, y, z).
Axes of the slice: x: 4 (x_hi: 2, x_lo: 2; x = x_hi * 2 + x_lo), y: 4, z: 8, core: 2. Of those that a mesh axis runs over, the one named last changes fastest.
Arguments:
- val_inputs: bfloat16 [256, 4096], P(None, 'tok'), may hold values from -6 to 6
- val_out_grad: bfloat16 [256, 4096], P(None, 'tok'), may hold values from -6 to 6
- w_gate: bfloat16 [4096, 14336], P('tok', 'hid'), may hold values from -0.09375 to 0.09375
- w_up: bfloat16 [4096, 14336], P('tok', 'hid'), may hold values from -0.09375 to 0.09375
- w_down: bfloat16 [14336, 4096], P('hid', 'tok'), may hold values from -0.046875 to 0.046875
- val_attn_inputs: bfloat16 [256, 4096], P('hid', 'tok'), may hold values from -6 to 6
- train_inputs: bfloat16 [163840, 4096], P(('hid', 'tok')), may hold values from -6 to 6
- train_grads: bfloat16 [163840, 4096], P(('hid', 'tok')), may hold values from -6 to 6
Outputs:
- influence: float32 [163840], P(('hid', 'tok'))
- val_grad: bfloat16 [256, 4096], P('hid', 'tok')
All inputs are finite; a program needn't handle non-finite values.
Results may differ from a plain program's by a relative error of at most 0.0036.
Values may be sent and summed in bfloat16 or wider, within the bound.
No kernel may reach another device: no remote copies, remote signals or barrier semaphores. Data moves between devices by JAX's collectives and lax.ppermute only.
A program may use at most 128 MiB of HBM per device.

v0:
```python
import math
import jax
import jax.numpy as jnp
from jax import lax
from jax.sharding import PartitionSpec as P


def dot_rows(left, right):
    return lax.dot_general(
        left, right, (((1,), (1,)), ((), ())), preferred_element_type=jnp.float32
    )


def act_grads(gate_pre, up_pre, hid_grad):
    logistic = jax.nn.sigmoid(gate_pre)
    grad_gate = (hid_grad * up_pre * logistic * (1.0 + gate_pre * (1.0 - logistic))).astype(
        jnp.bfloat16
    )
    grad_up = (hid_grad * gate_pre * logistic).astype(jnp.bfloat16)
    return (grad_gate, grad_up)


def pair_terms(train_in, train_gr, val_in, val_gr):
    in_gram = dot_rows(train_in, val_in)
    grad_gram = dot_rows(train_gr, val_gr)
    return jnp.sum(in_gram * grad_gram, axis=1)


def local(
    val_inputs, val_out_grad, w_gate, w_up, w_down, val_attn_inputs, train_inputs, train_grads
):
    hid_units = w_gate.shape[1]
    val_count = val_out_grad.shape[0]
    gate_pre = jnp.dot(val_inputs, w_gate, preferred_element_type=jnp.float32)
    up_pre = jnp.dot(val_inputs, w_up, preferred_element_type=jnp.float32)
    hid_grad = dot_rows(val_out_grad, w_down)
    sums = lax.psum_scatter(
        jnp.concatenate([gate_pre, up_pre, hid_grad], axis=1),
        "tok",
        scatter_dimension=0,
        tiled=True,
    )
    grad_gate, grad_up = act_grads(
        sums[:, :hid_units], sums[:, hid_units : 2 * hid_units], sums[:, 2 * hid_units :]
    )
    stacked = jnp.concatenate([grad_gate, grad_up], axis=1)
    piece = lax.all_gather(stacked, "tok", axis=0, tiled=True)
    dx_part = dot_rows(piece[:, :hid_units], w_gate) + dot_rows(piece[:, hid_units:], w_up)
    quarter = val_count // lax.axis_size("hid")
    first_row = lax.axis_index("hid") * quarter
    dx_rows = lax.psum_scatter(dx_part, "hid", scatter_dimension=0, tiled=True)
    own_rows = lax.dynamic_slice_in_dim(val_out_grad, first_row, quarter, 0)
    val_grad = (own_rows.astype(jnp.float32) + dx_rows).astype(jnp.bfloat16)
    attn_full, grad_full = (
        lax.all_gather(val_attn_inputs, "tok", axis=1, tiled=True),
        lax.all_gather(val_grad, "tok", axis=1, tiled=True),
    )
    total = pair_terms(
        train_inputs,
        train_grads,
        lax.all_gather(attn_full, "hid", axis=0, tiled=True),
        lax.all_gather(grad_full, "hid", axis=0, tiled=True),
    )
    influence = total / (train_inputs.shape[1] * math.sqrt(val_count))
    return (influence, val_grad)


def solution(mesh):
    placed = (
        P(None, "tok"),
        P(None, "tok"),
        P("tok", "hid"),
        P("tok", "hid"),
        P("hid", "tok"),
        P("hid", "tok"),
        P(("hid", "tok"), None),
        P(("hid", "tok"), None),
    )
    return jax.shard_map(
        local,
        mesh=mesh,
        in_specs=placed,
        out_specs=(P(("hid", "tok")), P("hid", "tok")),
        check_vma=False,
    )
```

profile of v0, /device:TPU:1, one launch (start us, length us, event | category | flops | bytes accessed | tf_op | source)
XLA Modules:
  0.0 1299.6 jit_solution(1939003087148605138)
XLA Ops:
  7.2 0.0 all-reduce.3.cloned.1.call-start
  7.3 1.8 fusion.13
  9.0 0.7 fusion.14
  9.7 0.7 fusion.15
  10.4 4.4 pad_maximum_fusion
  14.8 0.0 all-gather.9.cloned.1.call-start
  14.8 0.6 copy-done.7
  15.4 0.6 dynamic-slice
  16.7 697.3 %all-reduce.3.cloned.1.call-done = f32[256,10752]{1,0:T(8,128)} async-done(((f32[256,10752]{1,0:T(8,128)}), f32[256,10752]{1,0:T(8,128)}) %all-reduce.3.cloned.1.call-update) | async-done | bytes 11010064
  713.9 1.1 fusion.11
  715.1 0.6 maximum_bitcast_fusion
  715.7 0.0 reduce-scatter.2.cloned.1.call-start
  715.8 0.1 copy.14
  715.9 162.7 %all-gather.9.cloned.1.call-done = bf16[64,4,7168]{2,1,0:T(4,128)(2,1)} async-done(((bf16[1,4,7168]{2,1,0:T(4,128)(2,1)}), bf16[64,4,7168]{2,1,0:T(4,128)(2,1)}) %all-gather.9.cloned.1.call-update) | async-done | bytes 3670032 | tf_op jit(solution)/shard_map/all_gather | solution.py:47
  878.6 6.7 reshape.5
  885.3 2.1 fusion
  887.4 2.8 fusion.6
  890.2 0.0 all-gather.5.cloned.1.call-start
  890.3 155.9 %all_gather.15 = bf16[64,4096]{0,1:T(8,128)(2,1)S(1)} all-gather(bf16[64,64]{0,1:T(8,128)(2,1)S(1)} %copy.14), channel_id=1, replica_groups=mesh['hid'=4,'tok'=64] {'tok'}, dimensions={1}, use_global_device_ids=true | all-gather | bytes 532480 | tf_op jit(solution)/shard_map/all_gather | solution.py:55
  1046.2 1.1 copy.15
  1047.3 0.0 all-gather.7.cloned.1.call-start
  1047.4 0.1 constant_dynamic-slice_fusion
  1047.5 0.1 copy.19
  1047.6 0.0 reduce-scatter.2.cloned.1.call-done
  1047.6 0.8 add_convert_fusion
  1048.4 0.1 copy.17
  1048.4 153.2 %all_gather.18 = bf16[64,4096]{0,1:T(8,128)(2,1)S(1)} all-gather(bf16[64,64]{0,1:T(8,128)(2,1)S(1)} %copy.17), channel_id=1, replica_groups=mesh['hid'=4,'tok'=64] {'tok'}, dimensions={1}, use_global_device_ids=true | all-gather | bytes 532480 | tf_op jit(solution)/shard_map/all_gather | solution.py:56
  1201.7 1.1 copy.18
  1202.9 5.0 fusion.12
  1207.9 79.7 %all-gather.7.cloned.1.call-done = bf16[256,4096]{1,0:T(8,128)(2,1)} async-done(((bf16[64,4096]{1,0:T(8,128)(2,1)}), bf16[256,4096]{1,0:T(8,128)(2,1)}) %all-gather.7.cloned.1.call-update) | async-done | bytes 2097168 | tf_op jit(solution)/shard_map/all_gather | solution.py:62
  1287.5 5.0 fusion.5
  1292.5 0.6 broadcast_multiply_fusion
  (21 shorter events, 0.1 us)
Async XLA Ops:
  7.2 1.9 copy-start
  7.2 1.8 copy-start.3
  7.2 2.5 copy-start.1
  7.2 2.5 copy-start.4
  7.2 706.7 %all-reduce.3.cloned.1.call-start = ((), (), s32[]{:S(2)}) async-start(), calls=%async_computation.5 | async-start | bytes 22020096
  14.8 0.7 copy-start.7
  14.8 701.0 %copy-start.6 = (bf16[64,64]{1,0:T(8,128)(2,1)S(1)}, bf16[64,64]{1,0:T(8,128)(2,1)}, u32[]{:S(2)}) copy-start(bf16[64,64]{1,0:T(8,128)(2,1)} %param.13) | copy-start | bytes 24580
  14.8 863.8 %all-gather.9.cloned.1.call-start = ((), (), s32[]{:S(2)}) async-start(), calls=%async_computation.4 | async-start | bytes 3727360 | tf_op jit(solution)/shard_map/all_gather | solution.py:47
  715.7 331.8 %reduce-scatter.2.cloned.1.call-start = ((), (), s32[]{:S(2)}) async-start(), calls=%async_computation.2 | async-start | bytes 163840 | tf_op jit(solution)/shard_map/reduce_scatter | solution.py:51
  715.9 171.5 %copy-start.2 = (bf16[64,3584]{1,0:T(8,128)(2,1)S(1)}, bf16[64,3584]{1,0:T(8,128)(2,1)}, u32[]{:S(2)}) copy-start(bf16[64,3584]{1,0:T(8,128)(2,1)} %param.10) | copy-start | bytes 1376260
  890.2 312.6 %all-gather.5.cloned.1.call-start = ((), (), s32[]{:S(2)}) async-start(), calls=%async_computation.1 | async-start | bytes 2621440 | tf_op jit(solution)/shard_map/all_gather | solution.py:61
  1047.3 240.2 %all-gather.7.cloned.1.call-start = ((), (), s32[]{:S(2)}) async-start(), calls=%async_computation.3 | async-start | bytes 2621440 | tf_op jit(solution)/shard_map/all_gather | solution.py:62
  1048.4 159.5 %copy-start.5 = (bf16[64,64]{1,0:T(8,128)(2,1)}, bf16[64,64]{1,0:T(8,128)(2,1)S(1)}, u32[]{:S(2)}) copy-start(bf16[64,64]{1,0:T(8,128)(2,1)S(1)} %add_convert_fusion) | copy-start | bytes 24580
Sparse Core Ops, SparseCore 0:
  14.9 698.9 all-reduce.2
  717.4 161.1 all-gather.8
  890.4 20.3 reduce-scatter.1
  1047.4 56.4 all-gather.4
  1203.0 84.5 all-gather.6
where the time goes:
time: 1300 us
  waiting for transfers between devices  940 us (72%)
  blocking collectives  309 us (24%)
  matrix products  17.9 us (1%)
  between operations  14.6 us (1%)
    unnamed x6, waiting for transfers between devices  697 us
    all_gather x1, waiting for transfers between devices, local(): piece = lax.all_gather(stacked, 'tok', axis=0, tiled=True)  163 us
    all_gather x1, blocking collectives, local(): lax.all_gather(val_attn_inputs, 'tok', axis=1, tiled=True)  156 us
    all_gather x1, blocking collectives, local(): lax.all_gather(val_grad, 'tok', axis=1, tiled=True)  153 us
    all_gather x1, waiting for transfers between devices, local(): lax.all_gather(grad_full, 'hid', axis=0, tiled=True)  79.7 us
  transfers between devices with their start and end apart: 5, of which 3 were waited for; matrix products, arithmetic and copies ran while one was open for 1% of the time, Pallas kernels for 0%

commit v1 on v0

--- a/solution.py
+++ b/solution.py
@@ -53,7 +53,9 @@
     val_grad = (own_rows.astype(jnp.float32) + dx_rows).astype(jnp.bfloat16)
     attn_full, grad_full = (
         lax.all_gather(val_attn_inputs, "tok", axis=1, tiled=True),
-        lax.all_gather(val_grad, "tok", axis=1, tiled=True),
+        jnp.concatenate(
+            lax.all_to_all(jnp.stack([val_grad] * lax.axis_size("tok")), "tok", 0, 0), axis=1
+        ),
     )
     total = pair_terms(
         train_inputs,

time: 1300 us -> 1150 us (0.88)
  blocking collectives: 309 us -> 175 us
  waiting for transfers between devices: 940 us -> 925 us
    all_gather x1 -> x0, blocking collectives: 153 us -> none  [local(): lax.all_gather(val_grad, 'tok', axis=1, tiled=True)]
    all_gather x1, waiting for transfers between devices: 79.7 us -> 29.2 us  [local(): lax.all_gather(grad_full, 'hid', axis=0, tiled=True)]
    all_gather x1, waiting for transfers between devices: 0.02 us -> 36.1 us  [local(): lax.all_gather(attn_full, 'hid', axis=0, tiled=True)]
    all_to_all x0 -> x1, blocking collectives: none -> 19.4 us  [local(): lax.all_to_all(jnp.stack([val_grad] * lax.axis_size('tok')), 'tok', 0, 0)]
  transfers between devices with their start and end apart: 5 -> 5, of which waited for: 3 -> 4; matrix products, arithmetic and copies ran while one was open for 1% -> 1% of each run, Pallas kernels for 0% -> 0%
where the time goes in v1:
time: 1150 us
  waiting for transfers between devices  925 us (80%)
  blocking collectives  175 us (15%)
  matrix products  17.9 us (2%)
  between operations  14.6 us (1%)
  local copies, waits for them, and re-layouts  13.3 us (1%)
    unnamed x6, waiting for transfers between devices  697 us
    all_gather x1, waiting for transfers between devices, local(): piece = lax.all_gather(stacked, 'tok', axis=0, tiled=True)  163 us
    all_gather x1, blocking collectives, local(): lax.all_gather(val_attn_inputs, 'tok', axis=1, tiled=True)  156 us
    all_gather x1, waiting for transfers between devices, local(): lax.all_gather(attn_full, 'hid', axis=0, tiled=True)  36.1 us
    all_gather x1, waiting for transfers between devices, local(): lax.all_gather(grad_full, 'hid', axis=0, tiled=True)  29.2 us
  transfers between devices with their start and end apart: 5, of which 4 were waited for; matrix products, arithmetic and copies ran while one was open for 1% of the time, Pallas kernels for 0%

profile of v1, /device:TPU:1, one launch (start us, length us, event | category | flops | bytes accessed | tf_op | source)
XLA Modules:
  0.0 1154.2 jit_solution(1551896054513896411)
XLA Ops:
  7.3 1.8 fusion.13
  9.0 0.7 fusion.14
  9.7 0.7 fusion.15
  10.4 4.4 pad_maximum_fusion
  14.8 0.0 all-gather.9.cloned.1.call-start
  14.8 0.6 copy-done.7
  15.4 0.6 dynamic-slice
  16.7 697.3 %all-reduce.3.cloned.1.call-done = f32[256,10752]{1,0:T(8,128)} async-done(((f32[256,10752]{1,0:T(8,128)}), f32[256,10752]{1,0:T(8,128)}) %all-reduce.3.cloned.1.call-update) | async-done | bytes 11010064
  713.9 1.1 fusion.11
  715.1 0.6 maximum_bitcast_fusion
  715.8 0.1 copy.15
  715.9 162.7 %all-gather.9.cloned.1.call-done = bf16[64,4,7168]{2,1,0:T(4,128)(2,1)} async-done(((bf16[1,4,7168]{2,1,0:T(4,128)(2,1)}), bf16[64,4,7168]{2,1,0:T(4,128)(2,1)}) %all-gather.9.cloned.1.call-update) | async-done | bytes 3670032 | tf_op jit(solution)/shard_map/all_gather | solution.py:47
  878.6 6.7 reshape.15
  885.3 2.1 fusion
  887.4 2.8 fusion.6
  890.2 0.0 all-gather.5.cloned.1.call-start
  890.3 155.9 %all_gather.12 = bf16[64,4096]{0,1:T(8,128)(2,1)S(1)} all-gather(bf16[64,64]{0,1:T(8,128)(2,1)S(1)} %copy.15), channel_id=1, replica_groups=mesh['hid'=4,'tok'=64] {'tok'}, dimensions={1}, use_global_device_ids=true | all-gather | bytes 532480 | tf_op jit(solution)/shard_map/all_gather | solution.py:55
  1046.2 1.1 copy.16
  1047.4 0.1 constant_dynamic-slice_fusion
  1047.5 0.1 copy.19
  1047.6 0.8 add_convert_fusion
  1048.4 0.2 stack.2
  1048.6 0.7 reshape.17
  1049.3 19.4 %all_to_all.5 = bf16[64,2,2048]{2,1,0:T(2,128)(2,1)S(1)} all-to-all(bf16[64,2,2048]{2,1,0:T(2,128)(2,1)S(1)} %reshape.17), channel_id=1, replica_groups=mesh['hid'=4,'tok'=64] {'tok'}, dimensions={0} | all-to-all | bytes 1048576 | tf_op jit(solution)/shard_map/all_to_all | solution.py:57
  1068.7 0.7 reshape.18
  1069.4 0.7 copy.18
  1070.1 1.6 reshape.13
  1071.8 36.1 %all-gather.5.cloned.1.call-done = bf16[256,4096]{1,0:T(8,128)(2,1)} async-done(((bf16[64,4096]{1,0:T(8,128)(2,1)}), bf16[256,4096]{1,0:T(8,128)(2,1)}) %all-gather.5.cloned.1.call-update) | async-done | bytes 2097168 | tf_op jit(solution)/shard_map/all_gather | solution.py:63
  1107.9 5.0 fusion.12
  1112.9 29.2 %all-gather.7.cloned.1.call-done = bf16[256,4096]{1,0:T(8,128)(2,1)} async-done(((bf16[64,4096]{1,0:T(8,128)(2,1)}), bf16[256,4096]{1,0:T(8,128)(2,1)}) %all-gather.7.cloned.1.call-update) | async-done | bytes 2097168 | tf_op jit(solution)/shard_map/all_gather | solution.py:64
  1142.1 5.0 fusion.5
  1147.1 0.6 broadcast_multiply_fusion
  (24 shorter events, 0.3 us)
Async XLA Ops:
  7.2 1.9 copy-start
  7.2 1.8 copy-start.3
  7.2 2.5 copy-start.1
  7.2 2.5 copy-start.4
  7.2 706.7 %all-reduce.3.cloned.1.call-start = ((), (), s32[]{:S(2)}) async-start(), calls=%async_computation.6 | async-start | bytes 22020096
  14.8 0.7 copy-start.7
  14.8 701.0 %copy-start.6 = (bf16[64,64]{1,0:T(8,128)(2,1)S(1)}, bf16[64,64]{1,0:T(8,128)(2,1)}, u32[]{:S(2)}) copy-start(bf16[64,64]{1,0:T(8,128)(2,1)} %param.13) | copy-start | bytes 24580
  14.8 863.8 %all-gather.9.cloned.1.call-start = ((), (), s32[]{:S(2)}) async-start(), calls=%async_computation.5 | async-start | bytes 3727360 | tf_op jit(solution)/shard_map/all_gather | solution.py:47
  715.7 331.8 %reduce-scatter.2.cloned.1.call-start = ((), (), s32[]{:S(2)}) async-start(), calls=%async_computation.3 | async-start | bytes 163840 | tf_op jit(solution)/shard_map/reduce_scatter | solution.py:51
  715.9 171.5 %copy-start.2 = (bf16[64,3584]{1,0:T(8,128)(2,1)S(1)}, bf16[64,3584]{1,0:T(8,128)(2,1)}, u32[]{:S(2)}) copy-start(bf16[64,3584]{1,0:T(8,128)(2,1)} %param.10) | copy-start | bytes 1376260
  890.2 217.7 %all-gather.5.cloned.1.call-start = ((), (), s32[]{:S(2)}) async-start(), calls=%async_computation.2 | async-start | bytes 2621440 | tf_op jit(solution)/shard_map/all_gather | solution.py:63
  1047.3 94.8 %all-gather.7.cloned.1.call-start = ((), (), s32[]{:S(2)}) async-start(), calls=%async_computation.4 | async-start | bytes 2621440 | tf_op jit(solution)/shard_map/all_gather | solution.py:64
  1048.4 21.8 %copy-start.5 = (bf16[64,64]{1,0:T(8,128)(2,1)}, bf16[64,64]{1,0:T(8,128)(2,1)S(1)}, u32[]{:S(2)}) copy-start(bf16[64,64]{1,0:T(8,128)(2,1)S(1)} %add_convert_fusion) | copy-start | bytes 24580
Sparse Core Ops, SparseCore 0:
  14.9 698.9 all-reduce.2
  717.4 161.1 all-gather.8
  890.4 20.3 reduce-scatter.1
  1047.4 60.4 all-gather.4
  1109.6 32.5 all-gather.6

commit v2 on v0

--- a/solution.py
+++ b/solution.py
@@ -52,7 +52,7 @@
     own_rows = lax.dynamic_slice_in_dim(val_out_grad, first_row, quarter, 0)
     val_grad = (own_rows.astype(jnp.float32) + dx_rows).astype(jnp.bfloat16)
     attn_full, grad_full = (
-        lax.all_gather(val_attn_inputs, "tok", axis=1, tiled=True),
+        jnp.concatenate(lax.all_gather(val_attn_inputs, "tok"), axis=1),
         lax.all_gather(val_grad, "tok", axis=1, tiled=True),
     )
     total = pair_terms(

time: 1300 us -> 1300 us (level)
  no operation moved by 1% of the time
where the time goes in v2:
time: 1300 us
  waiting for transfers between devices  941 us (72%)
  blocking collectives  308 us (24%)
  matrix products  17.9 us (1%)
  between operations  14.6 us (1%)
    unnamed x6, waiting for transfers between devices  697 us
    all_gather x1, waiting for transfers between devices, local(): piece = lax.all_gather(stacked, 'tok', axis=0, tiled=True)  163 us
    all_gather x1, blocking collectives, local(): lax.all_gather(val_attn_inputs, 'tok')  156 us
    all_gather x1, blocking collectives, local(): lax.all_gather(val_grad, 'tok', axis=1, tiled=True)  152 us
    all_gather x1, waiting for transfers between devices, local(): lax.all_gather(grad_full, 'hid', axis=0, tiled=True)  80.4 us
  transfers between devices with their start and end apart: 5, of which 3 were waited for; matrix products, arithmetic and copies ran while one was open for 1% of the time, Pallas kernels for 0%

profile of v2, /device:TPU:1, one launch (start us, length us, event | category | flops | bytes accessed | tf_op | source)
XLA Modules:
  0.0 1300.8 jit_solution(13691281668593831053)
XLA Ops:
  7.2 0.0 all-reduce.3.cloned.1.call-start
  7.3 1.8 fusion.13
  9.0 0.7 fusion.14
  9.7 0.7 fusion.15
  10.4 4.4 pad_maximum_fusion
  14.8 0.0 all-gather.10.cloned.1.call-start
  14.8 0.6 copy-done.7
  15.4 0.6 dynamic-slice
  16.7 697.3 %all-reduce.3.cloned.1.call-done = f32[256,10752]{1,0:T(8,128)} async-done(((f32[256,10752]{1,0:T(8,128)}), f32[256,10752]{1,0:T(8,128)}) %all-reduce.3.cloned.1.call-update) | async-done | bytes 11010064
  713.9 1.1 fusion.11
  715.1 0.6 maximum_bitcast_fusion
  715.8 0.0 reduce-scatter.2.cloned.1.call-start
  715.8 162.8 %all-gather.10.cloned.1.call-done = bf16[64,4,7168]{2,1,0:T(4,128)(2,1)} async-done(((bf16[1,4,7168]{2,1,0:T(4,128)(2,1)}), bf16[64,4,7168]{2,1,0:T(4,128)(2,1)}) %all-gather.10.cloned.1.call-update) | async-done | bytes 3670032 | tf_op jit(solution)/shard_map/all_gather | solution.py:47
  878.6 6.7 reshape.14
  885.3 2.1 fusion
  887.5 2.8 fusion.6
  890.3 0.0 all-gather.6.cloned.1.call-start
  890.3 155.9 %all-gather = bf16[4096,64]{1,0:T(8,128)(2,1)S(1)} all-gather(bf16[64,64]{1,0:T(8,128)(2,1)S(1)} %copy-done.6), channel_id=2, replica_groups=mesh['hid'=4,'tok'=64] {'tok'}, dimensions={0}, use_global_device_ids=true | all-gather | bytes 532480 | tf_op jit(solution)/shard_map/all_gather | solution.py:55
  1046.2 0.7 copy.22
  1046.9 1.6 reshape.11
  1048.5 0.0 all-gather.8.cloned.1.call-start
  1048.6 0.1 constant_dynamic-slice_fusion
  1048.7 0.1 copy.20
  1048.8 0.8 add_convert_fusion
  1049.6 0.1 copy.18
  1049.7 152.4 %all_gather.22 = bf16[64,4096]{0,1:T(8,128)(2,1)S(1)} all-gather(bf16[64,64]{0,1:T(8,128)(2,1)S(1)} %copy.18), channel_id=1, replica_groups=mesh['hid'=4,'tok'=64] {'tok'}, dimensions={1}, use_global_device_ids=true | all-gather | bytes 532480 | tf_op jit(solution)/shard_map/all_gather | solution.py:56
  1202.1 1.1 copy.19
  1203.3 0.0 all-gather.6.cloned.1.call-done
  1203.3 5.0 fusion.12
  1208.3 80.4 %all-gather.8.cloned.1.call-done = bf16[256,4096]{1,0:T(8,128)(2,1)} async-done(((bf16[64,4096]{1,0:T(8,128)(2,1)}), bf16[256,4096]{1,0:T(8,128)(2,1)}) %all-gather.8.cloned.1.call-update) | async-done | bytes 2097168 | tf_op jit(solution)/shard_map/all_gather | solution.py:62
  1288.7 5.0 fusion.5
  1293.7 0.6 broadcast_multiply_fusion
  (21 shorter events, 0.1 us)
Async XLA Ops:
  7.2 1.9 copy-start
  7.2 1.8 copy-start.3
  7.2 2.5 copy-start.1
  7.2 2.5 copy-start.4
  7.2 706.7 %all-reduce.3.cloned.1.call-start = ((), (), s32[]{:S(2)}) async-start(), calls=%async_computation.5 | async-start | bytes 22020096
  14.8 0.7 copy-start.7
  14.8 863.8 %all-gather.10.cloned.1.call-start = ((), (), s32[]{:S(2)}) async-start(), calls=%async_computation.4 | async-start | bytes 3727360 | tf_op jit(solution)/shard_map/all_gather | solution.py:47
  715.7 171.7 %copy-start.2 = (bf16[64,3584]{1,0:T(8,128)(2,1)S(1)}, bf16[64,3584]{1,0:T(8,128)(2,1)}, u32[]{:S(2)}) copy-start(bf16[64,3584]{1,0:T(8,128)(2,1)} %param.10) | copy-start | bytes 1376260
  715.8 333.0 %reduce-scatter.2.cloned.1.call-start = ((), (), s32[]{:S(2)}) async-start(), calls=%async_computation.2 | async-start | bytes 163840 | tf_op jit(solution)/shard_map/reduce_scatter | solution.py:51
  885.3 5.0 copy-start.6
  890.3 313.0 %all-gather.6.cloned.1.call-start = ((), (), s32[]{:S(2)}) async-start(), calls=%async_computation.1 | async-start | bytes 2621440 | tf_op jit(solution)/shard_map/all_gather | solution.py:61
  1048.5 240.2 %all-gather.8.cloned.1.call-start = ((), (), s32[]{:S(2)}) async-start(), calls=%async_computation.3 | async-start | bytes 2621440 | tf_op jit(solution)/shard_map/all_gather | solution.py:62
  1049.6 158.7 %copy-start.5 = (bf16[64,64]{1,0:T(8,128)(2,1)}, bf16[64,64]{1,0:T(8,128)(2,1)S(1)}, u32[]{:S(2)}) copy-start(bf16[64,64]{1,0:T(8,128)(2,1)S(1)} %add_convert_fusion) | copy-start | bytes 24580
Sparse Core Ops, SparseCore 0:
  14.9 698.9 all-reduce.2
  717.4 161.1 all-gather.9
  890.4 20.3 reduce-scatter.1
  1048.7 56.4 all-gather.5
  1203.4 85.2 all-gather.7
